TPU v7x, 128 devices: a whole 4x4x4 slice. The times are simulated.
128 devices in a mesh: req: 32 (over y, z, core), tp: 4 (over x).
Axes of the slice: x: 4, y: 4, z: 4, core: 2. Of those that a mesh axis runs over, the one named last changes fastest.
Arguments:
- tokens: bfloat16 [512, 2048], P('req'), may hold values from -6 to 6
- lengths: int32 [512], P('req'), may hold values from 1 to 8192, 131072 in all
- pool_order: int32 [512], replicated, may hold values from 0 to 511, each once
- positions: int32 [512], P('req'), may hold values from 0 to 16383
- slot_mask: int32 [131072], P('req'), may hold values 0 or 1
- kv_cache: bfloat16 [131072, 2, 1024], P('req', None, 'tp'), may hold values from -420 to 420
- attn_gain: bfloat16 [2048], replicated, may hold values from 0.25 to 1.75
- w_query: bfloat16 [2048, 2048], P(None, 'tp'), may hold values from -0.125 to 0.125
- w_key: bfloat16 [2048, 1024], P(None, 'tp'), may hold values from -0.125 to 0.125
- w_value: bfloat16 [2048, 1024], P(None, 'tp'), may hold values from -0.125 to 0.125
- w_out: bfloat16 [2048, 2048], P('tp'), may hold values from -0.125 to 0.125
- ffn_gain: bfloat16 [2048], replicated, may hold values from 0.25 to 1.75
- w_gate: bfloat16 [2048, 4096], P(None, 'tp'), may hold values from -0.125 to 0.125
- w_up: bfloat16 [2048, 4096], P(None, 'tp'), may hold values from -0.125 to 0.125
- w_down: bfloat16 [4096, 2048], P('tp'), may hold values from -0.09375 to 0.09375
Outputs:
- hidden_out: float32 [512, 2048], P('req')
- new_kv: float32 [512, 2, 1024], P('req', None, 'tp')
Inputs may be any that keep to these rules, and one draw needn't show every extreme that they name: The lengths add up to 131072, so the requests' caches fill the pool end to end; the largest is exactly 8192. `pool_order`: each request appears exactly once.
All inputs are finite; a program needn't handle non-finite values. No bound on the sum of `lengths` or of `slot_mask` on one device may be relied on, other than what follows from the above.
Results may differ from a plain program's by a relative error of at most 0.013.
The roundings to bfloat16 on the way count: a program that leaves them out, or rounds other values in their place, can miss the bound.
Values may be sent and summed in bfloat16 or wider, within the bound.
A program may use at most 192 MiB of HBM per device.

v0:
```python
import math
import jax
import jax.numpy as jnp
from jax import lax
from jax.sharding import PartitionSpec as P

HEAD_DIM = 128
ROPE_BASE = 1000000.0
EPS = 1e-05
FLOOR = -1e30


def joined(part, axis, combine):
    gathered = jax.tree.map(lambda a: lax.all_gather(a, axis), part)

    def take(source):
        return jax.tree.map(lambda a: lax.dynamic_index_in_dim(a, source, 0, False), gathered)

    return lax.fori_loop(
        1, lax.axis_size(axis), lambda source, state: combine(state, take(source)), take(0)
    )


def rms_norm(rows, gain):
    mean_sq = jnp.mean(rows * rows, axis=-1, keepdims=True)
    return rows * lax.rsqrt(mean_sq + EPS) * gain.astype(jnp.float32)


def rotate(vectors, places):
    width = vectors.shape[-1]
    half = width // 2
    freq = ROPE_BASE ** (-(jnp.arange(half, dtype=jnp.float32) * 2.0) / width)
    angle = places.astype(jnp.float32)[:, None] * freq[None, :]
    cosine = jnp.cos(angle)[:, None, :]
    sine = jnp.sin(angle)[:, None, :]
    first = vectors[..., :half]
    second = vectors[..., half:]
    return jnp.concatenate(
        [first * cosine - second * sine, second * cosine + first * sine], axis=-1
    )


def combine_parts(first, second):
    peak = jnp.maximum(first[0], second[0])
    left = jnp.exp(first[0] - peak)
    right = jnp.exp(second[0] - peak)
    return (
        peak,
        first[1] * left + second[1] * right,
        first[2] * left[..., None] + second[2] * right[..., None],
    )


def per_device(
    tokens,
    lengths,
    pool_order,
    positions,
    slot_mask,
    kv_cache,
    attn_gain,
    w_query,
    w_key,
    w_value,
    w_out,
    ffn_gain,
    w_gate,
    w_up,
    w_down,
):
    count = tokens.shape[0]
    head_dim = HEAD_DIM
    kv_local = w_key.shape[1] // head_dim
    q_local = w_query.shape[1] // head_dim
    group = q_local // kv_local
    slot_count = kv_cache.shape[0]
    scale = 1.0 / math.sqrt(head_dim)
    highest = lax.Precision.HIGHEST
    all_lengths = lax.all_gather(lengths, "req", axis=0, tiled=True)
    total_reqs = all_lengths.shape[0]
    ordered = all_lengths[pool_order]
    ends = jnp.cumsum(ordered)
    base = lax.axis_index("req") * slot_count
    slot_ids = base + jnp.arange(slot_count, dtype=jnp.int32)
    place = jnp.searchsorted(ends, slot_ids, side="right")
    owner = pool_order[place]
    belongs = owner[:, None] == jnp.arange(total_reqs, dtype=jnp.int32)[None, :]
    belongs_f = belongs.astype(jnp.float32)
    rows = tokens.astype(jnp.float32)
    normed = rms_norm(rows, attn_gain).astype(jnp.bfloat16)
    query = rotate(
        jnp.dot(normed, w_query, preferred_element_type=jnp.float32).reshape(
            count, q_local, head_dim
        ),
        positions,
    ).astype(jnp.bfloat16)
    key_full = rotate(
        jnp.dot(normed, w_key, preferred_element_type=jnp.float32).reshape(
            count, kv_local, head_dim
        ),
        positions,
    )
    value_full = jnp.dot(normed, w_value, preferred_element_type=jnp.float32)
    new_kv = jnp.stack([key_full.reshape(count, kv_local * head_dim), value_full], axis=1)
    new_key = key_full.astype(jnp.bfloat16)
    new_value = value_full.astype(jnp.bfloat16)
    everyone = lax.all_gather(query.reshape(count, q_local * head_dim), "req", axis=0, tiled=True)
    picked = everyone[owner].reshape(slot_count, kv_local, group, head_dim)
    keys = kv_cache[:, 0, :].reshape(slot_count, kv_local, head_dim)
    values = kv_cache[:, 1, :].reshape(slot_count, kv_local, head_dim)
    scores = jnp.einsum("skgd,skd->skg", picked, keys, preferred_element_type=jnp.float32) * scale
    live = (slot_mask == 1)[:, None, None]
    scores = jnp.where(live, scores, FLOOR)
    peak_heads = []
    for head in range(kv_local):
        masked = jnp.where(belongs[:, :, None], scores[:, head, :][:, None, :], FLOOR)
        peak_heads.append(jnp.max(masked, axis=0))
    peak = jnp.stack(peak_heads, axis=1)
    weights = jnp.where(live, jnp.exp(scores - peak[owner]), 0.0)
    total = jnp.dot(
        belongs_f.T,
        weights.reshape(slot_count, kv_local * group),
        precision=highest,
        preferred_element_type=jnp.float32,
    ).reshape(total_reqs, kv_local, group)
    sum_heads = []
    for head in range(kv_local):
        spread = belongs_f[:, :, None] * weights[:, head, :][:, None, :]
        head_values = values[:, head, :].astype(jnp.float32)
        sum_heads.append(
            jnp.einsum(
                "srg,sd->rgd",
                spread,
                head_values,
                precision=highest,
                preferred_element_type=jnp.float32,
            )
        )
    summed = jnp.stack(sum_heads, axis=1)
    start = lax.axis_index("req") * count
    merged = joined((peak, total, summed), "req", combine_parts)
    own_peak = lax.dynamic_slice_in_dim(merged[0], start, count, 0)
    own_total = lax.dynamic_slice_in_dim(merged[1], start, count, 0)
    own_sum = lax.dynamic_slice_in_dim(merged[2], start, count, 0)
    own_query = query.reshape(count, kv_local, group, head_dim)
    own_score = (
        jnp.einsum("nkgd,nkd->nkg", own_query, new_key, preferred_element_type=jnp.float32) * scale
    )
    final_peak = jnp.maximum(own_peak, own_score)
    old_part = jnp.exp(own_peak - final_peak)
    new_part = jnp.exp(own_score - final_peak)
    denom = own_total * old_part + new_part
    numer = own_sum * old_part[..., None] + new_part[..., None] * new_value.reshape(
        count, kv_local, 1, head_dim
    ).astype(jnp.float32)
    context = (numer / denom[..., None]).reshape(count, q_local * head_dim).astype(jnp.bfloat16)
    partial_attn = jnp.dot(context, w_out, preferred_element_type=jnp.float32)
    mid = rows + lax.psum(partial_attn, "tp")
    normed_mid = rms_norm(mid, ffn_gain).astype(jnp.bfloat16)
    gate = jnp.dot(normed_mid, w_gate, preferred_element_type=jnp.float32)
    upper = jnp.dot(normed_mid, w_up, preferred_element_type=jnp.float32)
    act = (jax.nn.silu(gate) * upper).astype(jnp.bfloat16)
    down_part = jnp.dot(act, w_down, preferred_element_type=jnp.float32)
    hidden_out = mid + lax.psum(down_part, "tp")
    return (hidden_out, new_kv)


def solution(mesh):
    placed = (
        P("req", None),
        P("req"),
        P(),
        P("req"),
        P("req"),
        P("req", None, "tp"),
        P(),
        P(None, "tp"),
        P(None, "tp"),
        P(None, "tp"),
        P("tp", None),
        P(),
        P(None, "tp"),
        P(None, "tp"),
        P("tp", None),
    )
    return jax.shard_map(
        per_device,
        mesh=mesh,
        in_specs=placed,
        out_specs=(P("req", None), P("req", None, "tp")),
        check_vma=False,
    )
```

profile of v0, /device:TPU:0, one launch (start us, length us, event | category | flops | bytes accessed | tf_op | source)
XLA Modules:
  0.0 1126.8 jit_solution(8354011638535789150)
XLA Ops:
  12.5 18.3 %all-reduce = s32[512]{0:T(512)S(1)} all-reduce(s32[512]{0:T(512)S(1)} %dynamic-update-slice), channel_id=1, replica_groups=mesh['req'=32,'tp'=4] {'req'}, use_global_device_ids=true, to_apply=%add | all-reduce | flops 512 | bytes 4096
  36.3 259.8 %while.44 = (s32[]{:T(128)}, u32[4096]{0:T(1024)S(1)}, u32[4096]{0:T(1024)S(1)}, s32[512]{0:T(512)S(1)}, s32[]{:T(128)}, /*index=5*/s32[]{:T(128)}, s32[]{:T(128)}, s32[]{}) while((s32[]{:T(128)}, u32[4096]{0:T(1024)S(1)}, u32[4096]{0:T(1024)S(1)}, s32[512]{0:T(512)S(1)}, s32[]{:T(128)}, /*index=5*/s32[]{:T(128)}, s32[]{:T(128)}, ...), condition=%wide.region_3.4_spmd.clone, body=%wide.region_2.3_spmd.clone.sunk | while | flops 81924 | bytes 254065 | solution.py:85
  36.3 25.9 %gather_fusion = s32[4096]{0:T(1024)S(1)} fusion(s32[512]{0:T(512)S(1)} %get-tuple-element.479, u32[4096]{0:T(1024)S(1)} %broadcast_clamp_fusion.3), kind=kCustom, calls=%fused_computation.clone.clone.1 | custom fusion | bytes 49152 | tf_op jit(solution)/shard_map/jit(searchsorted)/jit(_searchsorted_scan_impl)/vmap(jit(_searchsorted_scan_impl))/while/body/eval_jaxpr/gather | solution.py:85
  62.3 25.9 %gather_fusion = s32[4096]{0:T(1024)S(1)} fusion(s32[512]{0:T(512)S(1)} %get-tuple-element.479, u32[4096]{0:T(1024)S(1)} %broadcast_clamp_fusion.3), kind=kCustom, calls=%fused_computation.clone.clone.1 | custom fusion | bytes 49152 | tf_op jit(solution)/shard_map/jit(searchsorted)/jit(_searchsorted_scan_impl)/vmap(jit(_searchsorted_scan_impl))/while/body/eval_jaxpr/gather | solution.py:85
  88.2 25.9 %gather_fusion = s32[4096]{0:T(1024)S(1)} fusion(s32[512]{0:T(512)S(1)} %get-tuple-element.479, u32[4096]{0:T(1024)S(1)} %broadcast_clamp_fusion.3), kind=kCustom, calls=%fused_computation.clone.clone.1 | custom fusion | bytes 49152 | tf_op jit(solution)/shard_map/jit(searchsorted)/jit(_searchsorted_scan_impl)/vmap(jit(_searchsorted_scan_impl))/while/body/eval_jaxpr/gather | solution.py:85
  114.2 25.9 %gather_fusion = s32[4096]{0:T(1024)S(1)} fusion(s32[512]{0:T(512)S(1)} %get-tuple-element.479, u32[4096]{0:T(1024)S(1)} %broadcast_clamp_fusion.3), kind=kCustom, calls=%fused_computation.clone.clone.1 | custom fusion | bytes 49152 | tf_op jit(solution)/shard_map/jit(searchsorted)/jit(_searchsorted_scan_impl)/vmap(jit(_searchsorted_scan_impl))/while/body/eval_jaxpr/gather | solution.py:85
  140.2 25.9 %gather_fusion = s32[4096]{0:T(1024)S(1)} fusion(s32[512]{0:T(512)S(1)} %get-tuple-element.479, u32[4096]{0:T(1024)S(1)} %broadcast_clamp_fusion.3), kind=kCustom, calls=%fused_computation.clone.clone.1 | custom fusion | bytes 49152 | tf_op jit(solution)/shard_map/jit(searchsorted)/jit(_searchsorted_scan_impl)/vmap(jit(_searchsorted_scan_impl))/while/body/eval_jaxpr/gather | solution.py:85
  166.2 25.9 %gather_fusion = s32[4096]{0:T(1024)S(1)} fusion(s32[512]{0:T(512)S(1)} %get-tuple-element.479, u32[4096]{0:T(1024)S(1)} %broadcast_clamp_fusion.3), kind=kCustom, calls=%fused_computation.clone.clone.1 | custom fusion | bytes 49152 | tf_op jit(solution)/shard_map/jit(searchsorted)/jit(_searchsorted_scan_impl)/vmap(jit(_searchsorted_scan_impl))/while/body/eval_jaxpr/gather | solution.py:85
  192.2 25.9 %gather_fusion = s32[4096]{0:T(1024)S(1)} fusion(s32[512]{0:T(512)S(1)} %get-tuple-element.479, u32[4096]{0:T(1024)S(1)} %broadcast_clamp_fusion.3), kind=kCustom, calls=%fused_computation.clone.clone.1 | custom fusion | bytes 49152 | tf_op jit(solution)/shard_map/jit(searchsorted)/jit(_searchsorted_scan_impl)/vmap(jit(_searchsorted_scan_impl))/while/body/eval_jaxpr/gather | solution.py:85
  218.1 25.9 %gather_fusion = s32[4096]{0:T(1024)S(1)} fusion(s32[512]{0:T(512)S(1)} %get-tuple-element.479, u32[4096]{0:T(1024)S(1)} %broadcast_clamp_fusion.3), kind=kCustom, calls=%fused_computation.clone.clone.1 | custom fusion | bytes 49152 | tf_op jit(solution)/shard_map/jit(searchsorted)/jit(_searchsorted_scan_impl)/vmap(jit(_searchsorted_scan_impl))/while/body/eval_jaxpr/gather | solution.py:85
  244.1 25.9 %gather_fusion = s32[4096]{0:T(1024)S(1)} fusion(s32[512]{0:T(512)S(1)} %get-tuple-element.479, u32[4096]{0:T(1024)S(1)} %broadcast_clamp_fusion.3), kind=kCustom, calls=%fused_computation.clone.clone.1 | custom fusion | bytes 49152 | tf_op jit(solution)/shard_map/jit(searchsorted)/jit(_searchsorted_scan_impl)/vmap(jit(_searchsorted_scan_impl))/while/body/eval_jaxpr/gather | solution.py:85
  270.1 25.9 %gather_fusion = s32[4096]{0:T(1024)S(1)} fusion(s32[512]{0:T(512)S(1)} %get-tuple-element.479, u32[4096]{0:T(1024)S(1)} %broadcast_clamp_fusion.3), kind=kCustom, calls=%fused_computation.clone.clone.1 | custom fusion | bytes 49152 | tf_op jit(solution)/shard_map/jit(searchsorted)/jit(_searchsorted_scan_impl)/vmap(jit(_searchsorted_scan_impl))/while/body/eval_jaxpr/gather | solution.py:85
  296.7 25.9 %gather_fusion.2 = s32[4096]{0:T(1024)S(1)} fusion(s32[512]{0:T(512)S(1)} %copy-done.1, s32[4096]{0:T(1024)S(1)} %fusion.38), kind=kCustom, calls=%fused_computation.2 | custom fusion | bytes 49152 | tf_op jit(solution)/shard_map/gather | solution.py:86
  328.4 22.5 %all_gather.22 = bf16[512,512]{1,0:T(8,128)(2,1)S(1)} all-gather(bf16[16,512]{1,0:T(8,128)(2,1)S(1)} %bitcast.112), channel_id=1, replica_groups=mesh['req'=32,'tp'=4] {'req'}, dimensions={0}, use_global_device_ids=true | all-gather | bytes 540672 | tf_op jit(solution)/shard_map/all_gather | solution.py:107
  351.0 17.3 %gather_fusion.3 = bf16[4096,512]{1,0:T(8,128)(2,1)} fusion(bf16[512,512]{1,0:T(8,128)(2,1)S(1)} %all_gather.22, s32[4096]{0:T(1024)S(1)} %broadcast_clamp_fusion.1), kind=kCustom, calls=%fused_computation.3 | custom fusion | bytes 8404992 | tf_op jit(solution)/shard_map/gather | solution.py:108
  425.5 14.4 %multiply_select_fusion = f32[4096,2,2]{2,1,0:T(2,128)S(1)} fusion(f32[4096,2,2]{2,1,0:T(2,128)S(1)} %bitcast.97, pred[4096]{0:T(1024)(128)(4,1)S(1)} %broadcast_compare_fusion), kind=kLoop, calls=%fused_computation.39 | loop fusion | flops 32768 | bytes 135168 | tf_op jit(solution)/shard_map/jit(_where)/select_n | solution.py:113
  463.9 28.3 %gather_fusion.4 = f32[4096,2,2]{2,1,0:T(2,128)} fusion(f32[512,2,2]{2,1,0:T(2,128)S(1)} %copy.93, s32[4096]{0:T(1024)S(1)} %broadcast_clamp_fusion.1), kind=kCustom, calls=%fused_computation.4 | custom fusion | bytes 147456 | tf_op jit(solution)/shard_map/gather | solution.py:119
  492.2 16.7 %exponential_select_fusion = f32[4096,2,2]{2,1,0:T(2,128)S(1)} fusion(f32[4096,2,2]{2,1,0:T(2,128)} %gather_fusion.4, pred[4096]{0:T(1024)(128)(4,1)S(1)} %broadcast_compare_fusion, f32[4096,2,2]{2,1,0:T(2,128)} %bitcast.98), kind=kLoop, calls=%fused_computation.38 | loop fusion | flops 65536 | bytes 200704 | tf_op jit(solution)/shard_map/jit(_where)/select_n | solution.py:119
  542.8 25.0 %all-gather = f32[16384,2,2]{0,2,1:T(2,128)S(1)} all-gather(f32[512,2,2]{0,2,1:T(2,128)S(1)} %pad_maximum_fusion.6), channel_id=2, replica_groups=mesh['req'=32,'tp'=4] {'req'}, dimensions={0}, use_global_device_ids=true | all-gather | bytes 270336 | tf_op jit(solution)/shard_map/all_gather | solution.py:14
  576.8 22.4 %all-gather.1 = f32[16384,2,2]{0,2,1:T(2,128)S(1)} all-gather(f32[512,2,2]{0,2,1:T(2,128)S(1)} %fusion.15), channel_id=3, replica_groups=mesh['req'=32,'tp'=4] {'req'}, dimensions={0}, use_global_device_ids=true | all-gather | bytes 270336 | tf_op jit(solution)/shard_map/all_gather | solution.py:14
  603.1 55.4 %all-gather.5.cloned.1.call-done = f32[16384,2,2,128]{3,0,2,1:T(8,128)} async-done(((f32[512,2,2,128]{3,0,2,1:T(8,128)}), f32[16384,2,2,128]{3,0,2,1:T(8,128)}) %all-gather.5.cloned.1.call-update) | async-done | bytes 33554448 | tf_op jit(solution)/shard_map/all_gather | solution.py:14
  661.5 362.1 %while.43 = (s32[]{:T(128)}, f32[512,2,2]{0,2,1:T(2,128)S(1)}, f32[512,2,2]{0,2,1:T(2,128)S(1)}, f32[512,2,2,128]{3,2,1,0:T(2,128)}, f32[32,512,2,2]{1,0,3,2:T(8...) while((s32[]{:T(128)}, f32[512,2,2]{0,2,1:T(2,128)S(1)}, ...), condition=%wide.region_8.9_spmd, body=%wide.region_7.8_spmd.sunk | while | flops 798725 | bytes 5390479 | solution.py:19
  1026.2 40.3 %all-reduce.4.cloned.1.call-done = f32[16,2048]{1,0:T(8,128)} async-done(((f32[16,2048]{1,0:T(8,128)}), f32[16,2048]{1,0:T(8,128)}) %all-reduce.4.cloned.1.call-update) | async-done | bytes 131088 | tf_op jit(solution)/shard_map/psum | solution.py:158
  1077.4 41.0 %all-reduce.6.cloned.1.call-done = f32[16,2048]{1,0:T(8,128)} async-done(((f32[16,2048]{1,0:T(8,128)}), f32[16,2048]{1,0:T(8,128)}) %all-reduce.6.cloned.1.call-update) | async-done | bytes 131088 | tf_op jit(solution)/shard_map/psum | solution.py:164
  (336 shorter events, 524.2 us)
Async XLA Ops:
  7.2 1017.8 %copy-start = (bf16[512,2048]{1,0:T(8,128)(2,1)S(1)}, bf16[512,2048]{1,0:T(8,128)(2,1)}, u32[]{:S(2)}) copy-start(bf16[512,2048]{1,0:T(8,128)(2,1)} %param.29) | copy-start | bytes 6291460
  7.2 651.3 %all-gather.5.cloned.1.call-start = ((), (), s32[]{:S(2)}) async-start(), calls=%async_computation.2 | async-start | bytes 34603008 | tf_op jit(solution)/shard_map/all_gather | solution.py:14
  296.0 0.7 copy-start.1
  322.6 5.1 copy-start.5
  322.6 5.0 copy-start.6
  425.5 14.5 %copy-start.3 = (f32[4096,2,1,2]{3,2,1,0:T(1,128)}, f32[4096,2,1,2]{3,2,1,0:T(1,128)S(1)}, u32[]{:S(2)}) copy-start(f32[4096,2,1,2]{3,2,1,0:T(1,128)S(1)} %fusion.57) | copy-start | bytes 196612
  508.9 5.1 copy-start.2
  518.5 11.7 %copy-start.4 = (bf16[4096,1,256]{0,2,1:T(8,128)(2,1)S(1)}, bf16[4096,1,256]{0,2,1:T(8,128)(2,1)}, u32[]{:S(2)}) copy-start(bf16[4096,1,256]{0,2,1:T(8,128)(2,1)} %copy.117) | copy-start | bytes 6291460
  542.8 523.6 %all-reduce.4.cloned.1.call-start = ((), (), s32[]{:S(2)}) async-start(), calls=%async_computation | async-start | bytes 262144 | tf_op jit(solution)/shard_map/psum | solution.py:158
  567.8 9.0 copy-start.8
  599.2 62.3 %slice-start = ((f32[16384,2,2]{0,2,1:T(2,128)}), f32[512,2,2]{0,2,1:T(2,128)S(1)}, s32[]{:S(2)}) async-start(f32[16384,2,2]{0,2,1:T(2,128)} %copy-done.8), calls=%async_computation.3 | async-start | bytes 16384 | tf_op jit(solution)/shard_map/jit(dynamic_index_in_dim)/dynamic_slice | solution.py:17
  661.5 364.6 %copy-start.9 = (bf16[2048]{0:T(1024)(128)(2,1)S(1)}, bf16[2048]{0:T(1024)(128)(2,1)}, u32[]{:S(2)}) copy-start(bf16[2048]{0:T(1024)(128)(2,1)} %param.30) | copy-start | bytes 12292
  1026.1 92.3 %all-reduce.6.cloned.1.call-start = ((), (), s32[]{:S(2)}) async-start(), calls=%async_computation.1 | async-start | bytes 262144 | tf_op jit(solution)/shard_map/psum | solution.py:164
  1071.3 47.1 %copy-start.7 = (f32[16,2048]{1,0:T(8,128)S(1)}, f32[16,2048]{1,0:T(8,128)}, u32[]{:S(2)}) copy-start(f32[16,2048]{1,0:T(8,128)} %all-reduce.4.cloned.1.call-done) | copy-start | bytes 393220
Sparse Core Ops, SparseCore 0:
  542.9 115.5 all-gather.4
  1026.2 40.1 all-reduce.3
  1076.8 41.5 all-reduce.5
where the time goes:
time: 1140 us; the launch traced here: 1130 us
  local copies, waits for them, and re-layouts  504 us (44%)
  other arithmetic  331 us (29%)
  waiting for transfers between devices  137 us (12%)
  blocking collectives  88.2 us (8%)
  matrix products  49.8 us (4%)
  between operations  15.1 us (1%)
    add x31, other arithmetic, combine_parts(): first[2] * left[..., None] + second[2] * right[..., None]  277 us
    gather x10, local copies, waits for them, and re-layouts, per_device(): place = jnp.searchsorted(ends, slot_ids, side='right')  259 us
    dynamic_slice x66, local copies, waits for them, and re-layouts, take(): lax.dynamic_index_in_dim(a, source, 0, False)  68.2 us
    all_gather x1, waiting for transfers between devices, joined(): gathered = jax.tree.map(lambda a: lax.all_gather(a, axis), part)  55.4 us
    all_gather x2, blocking collectives, joined(): gathered = jax.tree.map(lambda a: lax.all_gather(a, axis), part)  47.4 us
    psum x1, waiting for transfers between devices, per_device(): hidden_out = mid + lax.psum(down_part, 'tp')  41 us
    psum x1, waiting for transfers between devices, per_device(): mid = rows + lax.psum(partial_attn, 'tp')  40.3 us
    gather x1, local copies, waits for them, and re-layouts, per_device(): weights = jnp.where(live, jnp.exp(scores - peak[owner]), 0.0)  28.3 us
  transfers between devices with their start and end apart: 3, of which 3 were waited for; matrix products, arithmetic and copies ran while one was open for 1% of the time, Pallas kernels for 0%

commit v1 on v0

--- a/solution.py
+++ b/solution.py
@@ -1,3 +1,4 @@
+import functools
 import math
 import jax
 import jax.numpy as jnp
@@ -8,6 +9,14 @@
 ROPE_BASE = 1000000.0
 EPS = 1e-05
 FLOOR = -1e30
+
+
+def mark_links_in(mine_x, chip_axis):
+    current_arr = lax.all_gather(mine_x, axis_name=chip_axis)
+    return jnp.sum(current_arr, axis=0)
+
+
+_turn_values = functools.partial(mark_links_in, chip_axis="tp")
 
 
 def joined(part, axis, combine):
@@ -161,7 +170,7 @@
     upper = jnp.dot(normed_mid, w_up, preferred_element_type=jnp.float32)
     act = (jax.nn.silu(gate) * upper).astype(jnp.bfloat16)
     down_part = jnp.dot(act, w_down, preferred_element_type=jnp.float32)
-    hidden_out = mid + lax.psum(down_part, "tp")
+    hidden_out = mid + _turn_values(down_part)
     return (hidden_out, new_kv)
 
 

time: 1140 us -> 1110 us (0.974)
  waiting for transfers between devices: 137 us -> 95 us
  blocking collectives: 88.2 us -> 101 us
    psum x1 -> x0, waiting for transfers between devices: 41 us -> none  [per_device(): hidden_out = mid + lax.psum(down_part, 'tp')]
    all_gather x0 -> x1, blocking collectives: none -> 12.9 us  [mark_links_in(): current_arr = lax.all_gather(mine_x, axis_name=chip_axis)]
  transfers between devices with their start and end apart: 3 -> 2, of which waited for: 3 -> 2; matrix products, arithmetic and copies ran while one was open for 1% -> 1% of each run, Pallas kernels for 0% -> 0%
where the time goes in v1:
time: 1110 us; the launch traced here: 1100 us
  local copies, waits for them, and re-layouts  505 us (45%)
  other arithmetic  331 us (30%)
  blocking collectives  101 us (9%)
  waiting for transfers between devices  95 us (9%)
  matrix products  49.1 us (4%)
  between operations  15.4 us (1%)
    add x31, other arithmetic, combine_parts(): first[2] * left[..., None] + second[2] * right[..., None]  278 us
    gather x10, local copies, waits for them, and re-layouts, per_device(): place = jnp.searchsorted(ends, slot_ids, side='right')  259 us
    dynamic_slice x66, local copies, waits for them, and re-layouts, take(): lax.dynamic_index_in_dim(a, source, 0, False)  68.2 us
    all_gather x1, waiting for transfers between devices, joined(): gathered = jax.tree.map(lambda a: lax.all_gather(a, axis), part)  55.4 us
    all_gather x2, blocking collectives, joined(): gathered = jax.tree.map(lambda a: lax.all_gather(a, axis), part)  47.4 us
    psum x1, waiting for transfers between devices, per_device(): mid = rows + lax.psum(partial_attn, 'tp')  39.6 us
    gather x1, local copies, waits for them, and re-layouts, per_device(): weights = jnp.where(live, jnp.exp(scores - peak[owner]), 0.0)  28.5 us
    gather x1, local copies, waits for them, and re-layouts, per_device(): owner = pool_order[place]  25.9 us
  transfers between devices with their start and end apart: 2, of which 2 were waited for; matrix products, arithmetic and copies ran while one was open for 1% of the time, Pallas kernels for 0%

profile of v1, /device:TPU:0, one launch (start us, length us, event | category | flops | bytes accessed | tf_op | source)
XLA Modules:
  0.0 1097.2 jit_solution(18326767959702533367)
XLA Ops:
  12.5 18.3 %all-reduce = s32[512]{0:T(512)S(1)} all-reduce(s32[512]{0:T(512)S(1)} %dynamic-update-slice), channel_id=1, replica_groups=mesh['req'=32,'tp'=4] {'req'}, use_global_device_ids=true, to_apply=%add | all-reduce | flops 512 | bytes 4096
  36.3 259.8 %while.44 = (s32[]{:T(128)}, u32[4096]{0:T(1024)S(1)}, u32[4096]{0:T(1024)S(1)}, s32[512]{0:T(512)S(1)}, s32[]{:T(128)}, /*index=5*/s32[]{:T(128)}, s32[]{:T(128)}, s32[]{}) while((s32[]{:T(128)}, u32[4096]{0:T(1024)S(1)}, u32[4096]{0:T(1024)S(1)}, s32[512]{0:T(512)S(1)}, s32[]{:T(128)}, /*index=5*/s32[]{:T(128)}, s32[]{:T(128)}, ...), condition=%wide.region_3.4_spmd.clone, body=%wide.region_2.3_spmd.clone.sunk | while | flops 81924 | bytes 254065 | solution.py:94
  36.3 25.9 %gather_fusion = s32[4096]{0:T(1024)S(1)} fusion(s32[512]{0:T(512)S(1)} %get-tuple-element.479, u32[4096]{0:T(1024)S(1)} %broadcast_clamp_fusion.3), kind=kCustom, calls=%fused_computation.clone.clone.1 | custom fusion | bytes 49152 | tf_op jit(solution)/shard_map/jit(searchsorted)/jit(_searchsorted_scan_impl)/vmap(jit(_searchsorted_scan_impl))/while/body/eval_jaxpr/gather | solution.py:94
  62.3 25.9 %gather_fusion = s32[4096]{0:T(1024)S(1)} fusion(s32[512]{0:T(512)S(1)} %get-tuple-element.479, u32[4096]{0:T(1024)S(1)} %broadcast_clamp_fusion.3), kind=kCustom, calls=%fused_computation.clone.clone.1 | custom fusion | bytes 49152 | tf_op jit(solution)/shard_map/jit(searchsorted)/jit(_searchsorted_scan_impl)/vmap(jit(_searchsorted_scan_impl))/while/body/eval_jaxpr/gather | solution.py:94
  88.2 25.9 %gather_fusion = s32[4096]{0:T(1024)S(1)} fusion(s32[512]{0:T(512)S(1)} %get-tuple-element.479, u32[4096]{0:T(1024)S(1)} %broadcast_clamp_fusion.3), kind=kCustom, calls=%fused_computation.clone.clone.1 | custom fusion | bytes 49152 | tf_op jit(solution)/shard_map/jit(searchsorted)/jit(_searchsorted_scan_impl)/vmap(jit(_searchsorted_scan_impl))/while/body/eval_jaxpr/gather | solution.py:94
  114.2 25.9 %gather_fusion = s32[4096]{0:T(1024)S(1)} fusion(s32[512]{0:T(512)S(1)} %get-tuple-element.479, u32[4096]{0:T(1024)S(1)} %broadcast_clamp_fusion.3), kind=kCustom, calls=%fused_computation.clone.clone.1 | custom fusion | bytes 49152 | tf_op jit(solution)/shard_map/jit(searchsorted)/jit(_searchsorted_scan_impl)/vmap(jit(_searchsorted_scan_impl))/while/body/eval_jaxpr/gather | solution.py:94
  140.2 25.9 %gather_fusion = s32[4096]{0:T(1024)S(1)} fusion(s32[512]{0:T(512)S(1)} %get-tuple-element.479, u32[4096]{0:T(1024)S(1)} %broadcast_clamp_fusion.3), kind=kCustom, calls=%fused_computation.clone.clone.1 | custom fusion | bytes 49152 | tf_op jit(solution)/shard_map/jit(searchsorted)/jit(_searchsorted_scan_impl)/vmap(jit(_searchsorted_scan_impl))/while/body/eval_jaxpr/gather | solution.py:94
  166.2 25.9 %gather_fusion = s32[4096]{0:T(1024)S(1)} fusion(s32[512]{0:T(512)S(1)} %get-tuple-element.479, u32[4096]{0:T(1024)S(1)} %broadcast_clamp_fusion.3), kind=kCustom, calls=%fused_computation.clone.clone.1 | custom fusion | bytes 49152 | tf_op jit(solution)/shard_map/jit(searchsorted)/jit(_searchsorted_scan_impl)/vmap(jit(_searchsorted_scan_impl))/while/body/eval_jaxpr/gather | solution.py:94
  192.2 25.9 %gather_fusion = s32[4096]{0:T(1024)S(1)} fusion(s32[512]{0:T(512)S(1)} %get-tuple-element.479, u32[4096]{0:T(1024)S(1)} %broadcast_clamp_fusion.3), kind=kCustom, calls=%fused_computation.clone.clone.1 | custom fusion | bytes 49152 | tf_op jit(solution)/shard_map/jit(searchsorted)/jit(_searchsorted_scan_impl)/vmap(jit(_searchsorted_scan_impl))/while/body/eval_jaxpr/gather | solution.py:94
  218.1 25.9 %gather_fusion = s32[4096]{0:T(1024)S(1)} fusion(s32[512]{0:T(512)S(1)} %get-tuple-element.479, u32[4096]{0:T(1024)S(1)} %broadcast_clamp_fusion.3), kind=kCustom, calls=%fused_computation.clone.clone.1 | custom fusion | bytes 49152 | tf_op jit(solution)/shard_map/jit(searchsorted)/jit(_searchsorted_scan_impl)/vmap(jit(_searchsorted_scan_impl))/while/body/eval_jaxpr/gather | solution.py:94
  244.1 25.9 %gather_fusion = s32[4096]{0:T(1024)S(1)} fusion(s32[512]{0:T(512)S(1)} %get-tuple-element.479, u32[4096]{0:T(1024)S(1)} %broadcast_clamp_fusion.3), kind=kCustom, calls=%fused_computation.clone.clone.1 | custom fusion | bytes 49152 | tf_op jit(solution)/shard_map/jit(searchsorted)/jit(_searchsorted_scan_impl)/vmap(jit(_searchsorted_scan_impl))/while/body/eval_jaxpr/gather | solution.py:94
  270.1 25.9 %gather_fusion = s32[4096]{0:T(1024)S(1)} fusion(s32[512]{0:T(512)S(1)} %get-tuple-element.479, u32[4096]{0:T(1024)S(1)} %broadcast_clamp_fusion.3), kind=kCustom, calls=%fused_computation.clone.clone.1 | custom fusion | bytes 49152 | tf_op jit(solution)/shard_map/jit(searchsorted)/jit(_searchsorted_scan_impl)/vmap(jit(_searchsorted_scan_impl))/while/body/eval_jaxpr/gather | solution.py:94
  296.7 25.9 %gather_fusion.2 = s32[4096]{0:T(1024)S(1)} fusion(s32[512]{0:T(512)S(1)} %copy-done.1, s32[4096]{0:T(1024)S(1)} %fusion.38), kind=kCustom, calls=%fused_computation.2 | custom fusion | bytes 49152 | tf_op jit(solution)/shard_map/gather | solution.py:95
  328.4 22.5 %all_gather.28 = bf16[512,512]{1,0:T(8,128)(2,1)S(1)} all-gather(bf16[16,512]{1,0:T(8,128)(2,1)S(1)} %bitcast.114), channel_id=1, replica_groups=mesh['req'=32,'tp'=4] {'req'}, dimensions={0}, use_global_device_ids=true | all-gather | bytes 540672 | tf_op jit(solution)/shard_map/all_gather | solution.py:116
  350.9 17.3 %gather_fusion.3 = bf16[4096,512]{1,0:T(8,128)(2,1)} fusion(bf16[512,512]{1,0:T(8,128)(2,1)S(1)} %all_gather.28, s32[4096]{0:T(1024)S(1)} %broadcast_clamp_fusion.1), kind=kCustom, calls=%fused_computation.3 | custom fusion | bytes 8404992 | tf_op jit(solution)/shard_map/gather | solution.py:117
  425.4 14.4 %multiply_select_fusion = f32[4096,2,2]{2,1,0:T(2,128)S(1)} fusion(f32[4096,2,2]{2,1,0:T(2,128)S(1)} %bitcast.98, pred[4096]{0:T(1024)(128)(4,1)S(1)} %broadcast_compare_fusion), kind=kLoop, calls=%fused_computation.39 | loop fusion | flops 32768 | bytes 135168 | tf_op jit(solution)/shard_map/jit(_where)/select_n | solution.py:122
  463.8 28.5 %gather_fusion.4 = f32[4096,2,2]{2,1,0:T(2,128)} fusion(f32[512,2,2]{2,1,0:T(2,128)S(1)} %copy.93, s32[4096]{0:T(1024)S(1)} %broadcast_clamp_fusion.1), kind=kCustom, calls=%fused_computation.4 | custom fusion | bytes 147456 | tf_op jit(solution)/shard_map/gather | solution.py:128
  492.3 16.7 %exponential_select_fusion = f32[4096,2,2]{2,1,0:T(2,128)S(1)} fusion(f32[4096,2,2]{2,1,0:T(2,128)} %gather_fusion.4, pred[4096]{0:T(1024)(128)(4,1)S(1)} %broadcast_compare_fusion, f32[4096,2,2]{2,1,0:T(2,128)} %bitcast.99), kind=kLoop, calls=%fused_computation.38 | loop fusion | flops 65536 | bytes 200704 | tf_op jit(solution)/shard_map/jit(_where)/select_n | solution.py:128
  542.9 25.0 %all-gather = f32[16384,2,2]{0,2,1:T(2,128)S(1)} all-gather(f32[512,2,2]{0,2,1:T(2,128)S(1)} %pad_maximum_fusion.6), channel_id=2, replica_groups=mesh['req'=32,'tp'=4] {'req'}, dimensions={0}, use_global_device_ids=true | all-gather | bytes 270336 | tf_op jit(solution)/shard_map/all_gather | solution.py:23
  576.8 22.4 %all-gather.1 = f32[16384,2,2]{0,2,1:T(2,128)S(1)} all-gather(f32[512,2,2]{0,2,1:T(2,128)S(1)} %fusion.15), channel_id=3, replica_groups=mesh['req'=32,'tp'=4] {'req'}, dimensions={0}, use_global_device_ids=true | all-gather | bytes 270336 | tf_op jit(solution)/shard_map/all_gather | solution.py:23
  603.1 55.4 %all-gather.6.cloned.1.call-done = f32[16384,2,2,128]{3,0,2,1:T(8,128)} async-done(((f32[512,2,2,128]{3,0,2,1:T(8,128)}), f32[16384,2,2,128]{3,0,2,1:T(8,128)}) %all-gather.6.cloned.1.call-update) | async-done | bytes 33554448 | tf_op jit(solution)/shard_map/all_gather | solution.py:23
  661.6 362.5 %while.43 = (s32[]{:T(128)}, f32[512,2,2]{0,2,1:T(2,128)S(1)}, f32[512,2,2]{0,2,1:T(2,128)S(1)}, f32[512,2,2,128]{3,2,1,0:T(2,128)}, f32[32,512,2,2]{1,0,3,2:T(8...) while((s32[]{:T(128)}, f32[512,2,2]{0,2,1:T(2,128)S(1)}, ...), condition=%wide.region_8.9_spmd, body=%wide.region_7.8_spmd.sunk | while | flops 798725 | bytes 5390479 | solution.py:28
  1027.2 39.6 %all-reduce.3.cloned.1.call-done = f32[16,2048]{1,0:T(8,128)} async-done(((f32[16,2048]{1,0:T(8,128)}), f32[16,2048]{1,0:T(8,128)}) %all-reduce.3.cloned.1.call-update) | async-done | bytes 131088 | tf_op jit(solution)/shard_map/psum | solution.py:167
  1076.4 12.9 %all-gather.3 = f32[64,2048]{1,0:T(8,128)S(1)} all-gather(f32[16,2048]{1,0:T(8,128)S(1)} %fusion.26), channel_id=5, replica_groups=mesh['req'=32,'tp'=4] {'tp'}, dimensions={0}, use_global_device_ids=true | all-gather | bytes 655360 | tf_op jit(solution)/shard_map/all_gather | solution.py:15
  (335 shorter events, 522.8 us)
Async XLA Ops:
  7.2 1018.2 %copy-start = (bf16[512,2048]{1,0:T(8,128)(2,1)S(1)}, bf16[512,2048]{1,0:T(8,128)(2,1)}, u32[]{:S(2)}) copy-start(bf16[512,2048]{1,0:T(8,128)(2,1)} %param.29) | copy-start | bytes 6291460
  7.2 651.3 %all-gather.6.cloned.1.call-start = ((), (), s32[]{:S(2)}) async-start(), calls=%async_computation.1 | async-start | bytes 34603008 | tf_op jit(solution)/shard_map/all_gather | solution.py:23
  296.0 0.7 copy-start.1
  322.6 5.0 copy-start.5
  322.6 5.0 copy-start.6
  425.4 14.5 %copy-start.3 = (f32[4096,2,1,2]{3,2,1,0:T(1,128)}, f32[4096,2,1,2]{3,2,1,0:T(1,128)S(1)}, u32[]{:S(2)}) copy-start(f32[4096,2,1,2]{3,2,1,0:T(1,128)S(1)} %fusion.57) | copy-start | bytes 196612
  509.0 5.1 copy-start.2
  518.5 11.7 %copy-start.4 = (bf16[4096,1,256]{0,2,1:T(8,128)(2,1)S(1)}, bf16[4096,1,256]{0,2,1:T(8,128)(2,1)}, u32[]{:S(2)}) copy-start(bf16[4096,1,256]{0,2,1:T(8,128)(2,1)} %copy.117) | copy-start | bytes 6291460
  542.8 524.0 %all-reduce.3.cloned.1.call-start = ((), (), s32[]{:S(2)}) async-start(), calls=%async_computation | async-start | bytes 262144 | tf_op jit(solution)/shard_map/psum | solution.py:167
  567.9 9.0 copy-start.8
  599.3 62.3 %slice-start = ((f32[16384,2,2]{0,2,1:T(2,128)}), f32[512,2,2]{0,2,1:T(2,128)S(1)}, s32[]{:S(2)}) async-start(f32[16384,2,2]{0,2,1:T(2,128)} %copy-done.8), calls=%async_computation.2 | async-start | bytes 16384 | tf_op jit(solution)/shard_map/jit(dynamic_index_in_dim)/dynamic_slice | solution.py:26
  661.6 364.9 %copy-start.9 = (bf16[2048]{0:T(1024)(128)(2,1)S(1)}, bf16[2048]{0:T(1024)(128)(2,1)}, u32[]{:S(2)}) copy-start(bf16[2048]{0:T(1024)(128)(2,1)} %param.30) | copy-start | bytes 12292
  1071.7 17.7 %copy-start.7 = (f32[16,2048]{1,0:T(8,128)S(1)}, f32[16,2048]{1,0:T(8,128)}, u32[]{:S(2)}) copy-start(f32[16,2048]{1,0:T(8,128)} %all-reduce.3.cloned.1.call-done) | copy-start | bytes 393220
Sparse Core Ops, SparseCore 0:
  542.9 115.5 all-gather.5
  1026.6 40.1 all-reduce.2
